TPU v7x, 256 devices: a whole 4x4x8 slice. The times are simulated.
256 devices in a mesh: seq: 8 (over z), head: 4 (over y_hi, core), rep: 8 (over y_lo, x).
Axes of the slice: x: 4, y: 4 (y_hi: 2, y_lo: 2; y = y_hi * 2 + y_lo), z: 8, core: 2. Of those that a mesh axis runs over, the one named last changes fastest.
Arguments:
- queries: bfloat16 [8, 2048, 7168], P('rep', 'seq', 'head'), may hold values from -6 to 6
- new_keys: bfloat16 [8, 2048, 7168], P('rep', 'seq', 'head'), may hold values from -6 to 6
- new_values: bfloat16 [8, 2048, 7168], P('rep', 'seq', 'head'), may hold values from -4 to 4
- lengths: int32 [8, 4], P('rep'), may hold values from 1 to 1024, 2048 in all within a row
- offsets: int32 [8, 4], P('rep'), may hold values from 0 to 4095
- slot_map: int32 [8, 4], P('rep'), may hold values from 0 to 3, each once within a row
Outputs:
- attended: bfloat16 [8, 2048, 7168], P('rep', 'seq', 'head')
- key_cache: bfloat16 [8, 4, 1024, 7168], P('rep', 'head', None, 'seq')
- value_cache: bfloat16 [8, 4, 1024, 7168], P('rep', 'head', None, 'seq')
Inputs may be any that keep to these rules, and one draw needn't show every extreme that they name: `lengths`: each row sums to 2048; its first entry is the group's shared prompt; every row has one entry equal to 1024. `slot_map`: each row is a permutation of the group's requests.
All inputs are finite; a program needn't handle non-finite values.
Results may differ from a plain program's by a relative error of at most 0.011.
Values may be sent and summed in bfloat16 or wider, within the bound.
A program may use at most 128 MiB of HBM per device.

v0:
```python
import math
import jax
import jax.numpy as jnp
from jax import lax
from jax.sharding import PartitionSpec as P

HD = 224
NEG_FILL = -1e30
ROPE_BASE = 10000.0
KEY_BLOCK = 512


def rotate(source, places):
    full_width = source.shape[-1]
    half_width = full_width // 2
    inverse = jnp.power(
        jnp.float32(ROPE_BASE), -2.0 * jnp.arange(half_width, dtype=jnp.float32) / full_width
    )
    angles = places.astype(jnp.float32)[:, None] * inverse[None, :]
    cosine = jnp.cos(angles)[:, None, :]
    sine_terms = jnp.sin(angles)[:, None, :]
    first_part = source[..., :half_width].astype(jnp.float32)
    second_part = source[..., half_width:].astype(jnp.float32)
    rotated = jnp.concatenate(
        [
            first_part * cosine - second_part * sine_terms,
            second_part * cosine + first_part * sine_terms,
        ],
        axis=-1,
    )
    return rotated.astype(jnp.bfloat16)


def token_request(token_ids, ends_at):
    return jnp.sum((token_ids[:, None] >= ends_at[None, :]).astype(jnp.int32), axis=1)


def lookup_rows(request, lookup):
    matches = request[:, None] == jnp.arange(lookup.shape[0], dtype=jnp.int32)[None, :]
    return jnp.sum(jnp.where(matches, lookup[None, :], 0), axis=1)


def empty_state(head_count, row_count):
    return (
        jnp.full((head_count, row_count), NEG_FILL, jnp.float32),
        jnp.zeros((head_count, row_count), jnp.float32),
        jnp.zeros((head_count, row_count, HD), jnp.float32),
    )


def finish(running):
    row_best, row_total, summed = running
    head_count, row_count, _ = summed.shape
    return (
        (summed / row_total[:, :, None])
        .transpose(1, 0, 2)
        .reshape(row_count, head_count * HD)
        .astype(jnp.bfloat16)
    )


def update(
    running, query_token_rows, query_tok, query_req, key_rows, value_rows, key_start, ends_at
):
    row_count = key_rows.shape[0]
    head_count = query_token_rows.shape[1]
    key_token_index = key_start + jnp.arange(row_count, dtype=jnp.int32)
    key_req = token_request(key_token_index, ends_at)
    same_request = (key_req[None, :] == query_req[:, None]) & (
        key_token_index[None, :] <= query_tok[:, None]
    )
    prompt_keys = (key_req[None, :] == 0) & (query_req[:, None] != 0)
    allowed = same_request | prompt_keys
    row_best, row_total, summed = running
    key_head_stack = key_rows.reshape(row_count, head_count, HD)
    value_heads = value_rows.reshape(row_count, head_count, HD)
    scores = jnp.einsum(
        "ezq,izq->zei", query_token_rows, key_head_stack, preferred_element_type=jnp.float32
    ) * (1.0 / math.sqrt(HD))
    scores = jnp.where(allowed[None], scores, NEG_FILL)
    best_new = jnp.maximum(row_best, jnp.max(scores, axis=2))
    factor = jnp.exp(row_best - best_new)
    weights = jnp.where(allowed[None], jnp.exp(scores - best_new[:, :, None]), 0.0)
    total_new = row_total * factor + jnp.sum(weights, axis=2)
    mixed = jnp.einsum(
        "eva,ael->evl",
        weights.astype(jnp.bfloat16),
        value_heads,
        preferred_element_type=jnp.float32,
    )
    return (best_new, total_new, summed * factor[:, :, None] + mixed)


def per_device(queries, new_keys, new_values, lengths, offsets, slot_map):
    tok_dev = queries.shape[1]
    local_cols = queries.shape[2]
    head_count = local_cols // HD
    tokens_total = tok_dev * lax.axis_size("seq")
    cache_len = tokens_total // 2
    lengths_row = lengths[0]
    offsets_row = offsets[0]
    slots_row = slot_map[0]
    request_count = lengths_row.shape[0]
    ends_at = jnp.cumsum(lengths_row)
    begins = ends_at - lengths_row
    token_ids = lax.axis_index("seq") * tok_dev + jnp.arange(tok_dev, dtype=jnp.int32)
    request = token_request(token_ids, ends_at)
    places = lookup_rows(request, offsets_row) + token_ids - lookup_rows(request, begins)
    rot_queries = rotate(queries[0].reshape(tok_dev, head_count, HD), places)
    rot_keys = rotate(new_keys[0].reshape(tok_dev, head_count, HD), places).reshape(
        tok_dev, local_cols
    )
    value_rows = new_values[0]
    key_rows = lax.all_gather(rot_keys, "seq", axis=0, tiled=True)
    piece_values = lax.all_gather(value_rows, "seq", axis=0, tiled=True)
    row_count = key_rows.shape[0]

    def key_step(key_index, state_in):
        first_row = key_index * KEY_BLOCK
        return update(
            state_in,
            rot_queries,
            token_ids,
            request,
            lax.dynamic_slice_in_dim(key_rows, first_row, KEY_BLOCK, 0),
            lax.dynamic_slice_in_dim(piece_values, first_row, KEY_BLOCK, 0),
            first_row,
            ends_at,
        )

    finished = lax.fori_loop(0, row_count // KEY_BLOCK, key_step, empty_state(head_count, tok_dev))
    attended = finish(finished)
    stacked = jnp.stack([rot_keys, value_rows])
    my_slot = lax.axis_index("head")
    request_ids = jnp.arange(request_count, dtype=jnp.int32)
    owner = jnp.sum(jnp.where(slots_row == my_slot, request_ids, 0))
    owner_begin = jnp.sum(jnp.where(request_ids == owner, begins, 0))
    slot_of = lookup_rows(request, slots_row)
    member = slot_of[None, :] == request_ids[:, None]
    buckets = jnp.where(member[None, :, :, None], stacked[:, None], jnp.zeros((), jnp.bfloat16))
    moved = lax.all_to_all(
        lax.all_to_all(buckets, "head", split_axis=1, concat_axis=3, tiled=True),
        "seq",
        split_axis=3,
        concat_axis=2,
        tiled=True,
    )
    padded = jnp.concatenate(
        [moved, jnp.zeros((2, 1, cache_len, moved.shape[3]), jnp.bfloat16)], axis=2
    )
    window = lax.dynamic_slice_in_dim(padded, owner_begin, cache_len, 2)
    return (attended[None], window[0:1], window[1:2])


def solution(mesh):
    in_specs = (
        P("rep", "seq", "head"),
        P("rep", "seq", "head"),
        P("rep", "seq", "head"),
        P("rep", None),
        P("rep", None),
        P("rep", None),
    )
    out_specs = (
        P("rep", "seq", "head"),
        P("rep", "head", None, "seq"),
        P("rep", "head", None, "seq"),
    )
    return jax.shard_map(
        per_device, mesh=mesh, in_specs=in_specs, out_specs=out_specs, check_vma=False
    )
```

profile of v0, /device:TPU:96, one launch (start us, length us, event | category | flops | bytes accessed | tf_op | source)
XLA Modules:
  0.0 385.8 jit_solution(3452643616625133445)
XLA Ops:
  7.2 0.0 all-gather.4.cloned.1.call-start
  7.3 0.9 reduce-window.4
  8.1 0.7 fusion.29
  8.8 1.5 copy.46
  10.3 0.1 convert_reduce_fusion.1
  10.4 0.8 select_reduce_fusion
  11.1 0.5 multiply_cosine_fusion
  11.6 0.3 fusion.21
  11.9 1.0 maximum_convert_fusion
  12.9 0.0 all-gather.4.cloned.1.call-update
  12.9 0.0 all-gather.6.cloned.1.call-start
  13.0 1.3 copy.48
  14.3 0.0 all-gather.6.cloned.1.call-update
  14.3 0.6 copy.49
  14.9 1.4 pad_maximum_fusion
  16.3 2.8 copy.50
  19.1 3.4 broadcast_select_fusion
  22.6 5.6 %all-to-all-start = ((bf16[2,4,256,1792]{2,3,0,1:T(8,128)(2,1)}), bf16[2,4,256,1792]{2,3,0,1:T(8,128)(2,1)}, u32[]{:S(2)}, u32[]{:S(2)}) async-start(bf16[2,4,256,1792]{2,3,0,1:T(8,128)(2,1)} %broadcast_select_fusion), calls=%async_computation | async-start | bytes 14680064 | tf_op jit(solution)/shard_map/all_to_all | solution.py:142
  28.2 0.5 copy.47
  28.8 0.7 fusion.27
  29.5 0.0 copy-done.4
  29.5 1.3 fusion.28
  32.6 0.3 fusion.24
  32.9 0.1 pad_maximum_fusion.1
  33.0 78.6 %all-to-all-done = bf16[2,4,256,1792]{2,3,0,1:T(8,128)(2,1)} async-done(((bf16[2,4,256,1792]{2,3,0,1:T(8,128)(2,1)}), bf16[2,4,256,1792]{2,3,0,1:T(8,128)(2,1)}, u32[]{:S(2)}, u32[]{:S(2)}) %all-to-all-start) | async-done | bytes 7340064 | tf_op jit(solution)/shard_map/all_to_all | solution.py:142
  111.6 3.6 copy.51
  115.2 47.2 %copy.52 = bf16[2,1,256,7168]{2,0,1,3:T(2,128)(2,1)} copy(bf16[2,1,256,7168]{2,3,0,1:T(8,128)(2,1)S(1)} %bitcast.73) | data formatting | bytes 14680064 | tf_op jit(solution)/shard_map/all_to_all | solution.py:142
  162.3 7.7 %all-to-all-start.1 = ((bf16[2,1,256,7168]{2,0,1,3:T(2,128)(2,1)}), bf16[2,1,256,7168]{2,0,1,3:T(2,128)(2,1)}, u32[]{:S(2)}, u32[]{:S(2)}) async-start(bf16[2,1,256,7168]{2,0,1,3:T(2,128)(2,1)} %copy.52), calls=%async_computation.1 | async-start | bytes 14680064 | tf_op jit(solution)/shard_map/all_to_all | solution.py:141
  170.0 106.1 %all-gather.6.cloned.1.call-done = bf16[1,2048,1792]{1,2,0:T(8,128)(2,1)} async-done(((bf16[1,256,1792]{1,2,0:T(8,128)(2,1)}), bf16[1,2048,1792]{1,2,0:T(8,128)(2,1)}) %all-gather.6.cloned.1.call-update) | async-done | bytes 7340048 | tf_op jit(solution)/shard_map/all_gather | solution.py:115
  276.2 51.9 %while.18 = (s32[]{:T(128)}, f32[8,256]{1,0:T(8,128)S(1)}, f32[8,256]{1,0:T(8,128)S(1)}, f32[8,256,224]{1,2,0:T(8,128)}, s32[4]{0:T(128)S(1)}, /*index=5*/s32[25...) while((s32[]{:T(128)}, f32[8,256]{1,0:T(8,128)S(1)}, ...), condition=%wide.region_8.9_spmd.clone, body=%wide.region_4.8_spmd.clone.sunk | while | flops 955204608 | bytes 45631228 | solution.py:131
  276.2 0.1 convert_reduce_fusion.3
  276.3 0.3 and_or_fusion.2
  276.6 2.3 constant_dynamic-slice_fusion.3
  278.9 3.1 fusion.45
  281.9 3.3 fusion.46
  285.3 0.1 copy-done
  285.4 2.6 fusion.48
  288.0 0.1 convert_reduce_fusion.3
  288.1 0.3 and_or_fusion.2
  288.4 2.3 constant_dynamic-slice_fusion.3
  290.7 3.1 fusion.45
  293.8 3.3 fusion.46
  297.2 0.1 copy-done
  297.2 4.1 %fusion.48 = f32[8,256,224]{1,2,0:T(8,128)} fusion(f32[8,256,224]{1,2,0:T(8,128)} %get-tuple-element.350, bf16[512,8,224]{0,2,1:T(8,128)(2,1)S(1)} %bitcast.71, f32[8,512,256]{2,1,0:T(8,128)S(1)} %copy-done, f32[8,256]{1,0:T(8,128)S(1)} %select_maximum_fusion.2, pred[256,512]{0,1:T(8,128)(4,1)S(1)} %and_or_fusion.2, ...), kind=kOutput, calls=%fused_computation.13.clone.1 | convolution fusion | flops 476381184 | bytes 9846785 | tf_op jit(solution)/shard_map/while/body/eval_jaxpr/eva,ael->evl/dot_general | solution.py:85
  301.4 0.1 convert_reduce_fusion.3
  301.5 0.3 and_or_fusion.2
  301.8 2.3 constant_dynamic-slice_fusion.3
  304.1 3.1 fusion.45
  307.2 3.3 fusion.46
  310.5 0.1 copy-done
  310.6 4.1 %fusion.48 = f32[8,256,224]{1,2,0:T(8,128)} fusion(f32[8,256,224]{1,2,0:T(8,128)} %get-tuple-element.350, bf16[512,8,224]{0,2,1:T(8,128)(2,1)S(1)} %bitcast.71, f32[8,512,256]{2,1,0:T(8,128)S(1)} %copy-done, f32[8,256]{1,0:T(8,128)S(1)} %select_maximum_fusion.2, pred[256,512]{0,1:T(8,128)(4,1)S(1)} %and_or_fusion.2, ...), kind=kOutput, calls=%fused_computation.13.clone.1 | convolution fusion | flops 476381184 | bytes 9846785 | tf_op jit(solution)/shard_map/while/body/eval_jaxpr/eva,ael->evl/dot_general | solution.py:85
  314.7 0.1 convert_reduce_fusion.3
  314.8 0.3 and_or_fusion.2
  315.1 2.3 constant_dynamic-slice_fusion.3
  317.4 3.1 fusion.45
  320.5 3.3 fusion.46
  323.9 0.1 copy-done
  323.9 4.1 %fusion.48 = f32[8,256,224]{1,2,0:T(8,128)} fusion(f32[8,256,224]{1,2,0:T(8,128)} %get-tuple-element.350, bf16[512,8,224]{0,2,1:T(8,128)(2,1)S(1)} %bitcast.71, f32[8,512,256]{2,1,0:T(8,128)S(1)} %copy-done, f32[8,256]{1,0:T(8,128)S(1)} %select_maximum_fusion.2, pred[256,512]{0,1:T(8,128)(4,1)S(1)} %and_or_fusion.2, ...), kind=kOutput, calls=%fused_computation.13.clone.1 | convolution fusion | flops 476381184 | bytes 9846785 | tf_op jit(solution)/shard_map/while/body/eval_jaxpr/eva,ael->evl/dot_general | solution.py:85
  328.1 1.6 divide_convert_fusion
  329.7 1.4 copy.55
  331.1 24.2 %all-to-all-done.1 = bf16[2,1,256,7168]{2,0,1,3:T(2,128)(2,1)} async-done(((bf16[2,1,256,7168]{2,0,1,3:T(2,128)(2,1)}), bf16[2,1,256,7168]{2,0,1,3:T(2,128)(2,1)}, u32[]{:S(2)}, u32[]{:S(2)}) %all-to-all-start.1) | async-done | bytes 7340064 | tf_op jit(solution)/shard_map/all_to_all | solution.py:141
  355.3 7.0 %copy.53 = bf16[2,1,256,7168]{2,3,0,1:T(8,128)(2,1)} copy(bf16[2,1,256,7168]{2,0,1,3:T(2,128)(2,1)} %all-to-all-done.1) | data formatting | bytes 14680064 | tf_op jit(solution)/shard_map/all_to_all | solution.py:141
  362.3 11.1 %copy.54 = bf16[2,1,8,256,896]{4,3,2,0,1:T(8,128)(2,1)} copy(bf16[2,1,8,256,896]{3,4,2,0,1:T(8,128)(2,1)} %bitcast.74) | data formatting | bytes 14680064 | tf_op jit(solution)/shard_map/all_to_all | solution.py:141
  373.4 5.6 %fusion.19 = (bf16[1,1,1024,896]{3,2,1,0:T(8,128)(2,1)}, bf16[1,1,1024,896]{3,2,1,0:T(8,128)(2,1)}) fusion(s32[]{:T(128)S(6)} %add.111, s32[]{:T(128)S(6)} %select_n.53, bf16[2,1,2048,896]{3,2,0,1:T(8,128)(2,1)} %bitcast.75), kind=kLoop, calls=%fused_computation.32 | loop fusion | bytes 11010056
  (49 shorter events, 0.2 us)
Async XLA Ops:
  7.2 5.8 %copy-start.2 = (bf16[1,256,1792]{2,1,0:T(8,128)(2,1)S(1)}, bf16[1,256,1792]{2,1,0:T(8,128)(2,1)}, u32[]{:S(2)}) copy-start(bf16[1,256,1792]{2,1,0:T(8,128)(2,1)} %param.10) | copy-start | bytes 2752516
  7.2 162.8 %all-gather.4.cloned.1.call-start = ((), (), s32[]{:S(2)}) async-start(), calls=%async_computation.2 | async-start | bytes 8257536 | tf_op jit(solution)/shard_map/all_gather | solution.py:114
  12.9 1.4 copy-start.1
  12.9 263.2 %all-gather.6.cloned.1.call-start = ((), (), s32[]{:S(2)}) async-start(), calls=%async_computation.3 | async-start | bytes 8257536 | tf_op jit(solution)/shard_map/all_gather | solution.py:115
  22.6 5.6 %copy-start.3 = (bf16[1,256,1792]{2,1,0:T(8,128)(2,1)S(1)}, bf16[1,256,1792]{2,1,0:T(8,128)(2,1)}, u32[]{:S(2)}) copy-start(bf16[1,256,1792]{2,1,0:T(8,128)(2,1)} %param.8) | copy-start | bytes 2752516
  22.6 6.2 %copy-start.5 = (s32[1,4]{1,0:T(1,128)S(1)}, s32[1,4]{1,0:T(1,128)}, u32[]{:S(2)}) copy-start(s32[1,4]{1,0:T(1,128)} %param.13) | copy-start | bytes 52
  22.6 6.9 %copy-start.4 = (s32[1,4]{1,0:T(1,128)S(1)}, s32[1,4]{1,0:T(1,128)}, u32[]{:S(2)}) copy-start(s32[1,4]{1,0:T(1,128)} %param.11) | copy-start | bytes 52
  22.6 89.0 %all-to-all-start = ((bf16[2,4,256,1792]{2,3,0,1:T(8,128)(2,1)}), bf16[2,4,256,1792]{2,3,0,1:T(8,128)(2,1)}, u32[]{:S(2)}, u32[]{:S(2)}) async-start(bf16[2,4,256,1792]{2,3,0,1:T(8,128)(2,1)} %broadcast_select_fusion), calls=%async_computation | async-start | bytes 14680064 | tf_op jit(solution)/shard_map/all_to_all | solution.py:142
  162.3 192.9 %all-to-all-start.1 = ((bf16[2,1,256,7168]{2,0,1,3:T(2,128)(2,1)}), bf16[2,1,256,7168]{2,0,1,3:T(2,128)(2,1)}, u32[]{:S(2)}, u32[]{:S(2)}) async-start(bf16[2,1,256,7168]{2,0,1,3:T(2,128)(2,1)} %copy.52), calls=%async_computation.1 | async-start | bytes 14680064 | tf_op jit(solution)/shard_map/all_to_all | solution.py:141
  281.9 3.4 copy-start
  293.8 3.4 copy-start
  307.1 3.4 copy-start
  320.5 3.4 copy-start
Sparse Core Ops, SparseCore 0:
  13.1 91.4 all-gather.3
  106.8 169.2 all-gather.5
where the time goes:
time: 387 us; the launch traced here: 386 us
  waiting for transfers between devices  209 us (54%)
  local copies, waits for them, and re-layouts  92 us (24%)
  other arithmetic  28 us (7%)
  matrix products  27.3 us (7%)
  between operations  16.1 us (4%)
  starting transfers between devices  13.3 us (3%)
    all_gather x1, waiting for transfers between devices, per_device(): piece_values = lax.all_gather(value_rows, 'seq', axis=0, tiled=True)  106 us
    all_to_all x1, waiting for transfers between devices, per_device(): lax.all_to_all(buckets, 'head', split_axis=1, concat_axis=3, tiled=True)  78.6 us
    all_to_all x2, local copies, waits for them, and re-layouts, per_device(): lax.all_to_all(buckets, 'head', split_axis=1, concat_axis=3, tiled=True)  50.7 us
    all_to_all x1, waiting for transfers between devices, per_device(): lax.all_to_all(lax.all_to_all(buckets, 'head', split_axis=1, concat_axis=...  24.2 us
    all_to_all x2, local copies, waits for them, and re-layouts, per_device(): lax.all_to_all(lax.all_to_all(buckets, 'head', split_axis=1, concat_axis=...  18.1 us
    dot_general x4, matrix products, update(): jnp.einsum('eva,ael->evl', weights.astype(jnp.bfloat16), value_heads, pre...  15 us
    reduce_sum x4, other arithmetic, update(): total_new = row_total * factor + jnp.sum(weights, axis=2)  13.3 us
    dot_general x4, matrix products, update(): jnp.einsum('ezq,izq->zei', query_token_rows, key_head_stack, preferred_el...  12.3 us
  transfers between devices with their start and end apart: 4, of which 3 were waited for; matrix products, arithmetic and copies ran while one was open for 31% of the time, Pallas kernels for 0%

commit v1 on v0

--- a/solution.py
+++ b/solution.py
@@ -112,7 +112,9 @@
     )
     value_rows = new_values[0]
     key_rows = lax.all_gather(rot_keys, "seq", axis=0, tiled=True)
-    piece_values = lax.all_gather(value_rows, "seq", axis=0, tiled=True)
+    piece_values = jnp.concatenate(
+        lax.all_to_all(jnp.stack([value_rows] * lax.axis_size("seq")), "seq", 0, 0), 0
+    )
     row_count = key_rows.shape[0]
 
     def key_step(key_index, state_in):

time: 387 us -> 546 us (1.41); the launches traced: 386 us -> 539 us
  waiting for transfers between devices: 209 us -> 309 us
  local copies, waits for them, and re-layouts: 92 us -> 118 us
  starting transfers between devices: 13.3 us -> 34.5 us
  matrix products: 27.3 us -> 35.3 us
    all_to_all x0 -> x1, waiting for transfers between devices: none -> 151 us  [per_device(): lax.all_to_all(jnp.stack([value_rows] * lax.axis_size('seq')), 'seq', 0, 0)]
    all_gather x1 -> x0, waiting for transfers between devices: 106 us -> none  [per_device(): piece_values = lax.all_gather(value_rows, 'seq', axis=0, tiled=True)]
    all_to_all x1, waiting for transfers between devices: 24.2 us -> 73.8 us  [per_device(): lax.all_to_all(lax.all_to_all(buckets, 'head', split_axis=1, concat_axis=...]
    all_to_all x1, starting transfers between devices: 7.67 us -> 21.1 us  [per_device(): lax.all_to_all(lax.all_to_all(buckets, 'head', split_axis=1, concat_axis=...]
    all_to_all x0 -> x1, local copies, waits for them, and re-layouts: none -> 10.1 us  [per_device(): lax.all_to_all(jnp.stack([value_rows] * lax.axis_size('seq')), 'seq', 0, 0)]
    all_to_all x0 -> x1, starting transfers between devices: none -> 7.79 us  [per_device(): lax.all_to_all(jnp.stack([value_rows] * lax.axis_size('seq')), 'seq', 0, 0)]
    dot_general x4, matrix products: 15 us -> 22.7 us  [update(): jnp.einsum('eva,ael->evl', weights.astype(jnp.bfloat16), value_heads, pre...]
    dynamic_slice x4 -> x8, local copies, waits for them, and re-layouts: 9.24 us -> 15.8 us  [key_step(): lax.dynamic_slice_in_dim(piece_values, first_row, KEY_BLOCK, 0)]
  transfers between devices with their start and end apart: 4 -> 4, of which waited for: 3 -> 3; matrix products, arithmetic and copies ran while one was open for 31% -> 26% of each run, Pallas kernels for 0% -> 0%
where the time goes in v1:
time: 546 us; the launch traced here: 539 us
  waiting for transfers between devices  309 us (57%)
  local copies, waits for them, and re-layouts  118 us (22%)
  matrix products  35.3 us (6%)
  starting transfers between devices  34.5 us (6%)
  other arithmetic  26.4 us (5%)
  between operations  16.1 us (3%)
    all_to_all x1, waiting for transfers between devices, per_device(): lax.all_to_all(jnp.stack([value_rows] * lax.axis_size('seq')), 'seq', 0, 0)  151 us
    all_to_all x1, waiting for transfers between devices, per_device(): lax.all_to_all(buckets, 'head', split_axis=1, concat_axis=3, tiled=True)  82.9 us
    all_to_all x1, waiting for transfers between devices, per_device(): lax.all_to_all(lax.all_to_all(buckets, 'head', split_axis=1, concat_axis=...  73.8 us
    all_to_all x2, local copies, waits for them, and re-layouts, per_device(): lax.all_to_all(buckets, 'head', split_axis=1, concat_axis=3, tiled=True)  50.7 us
    dot_general x4, matrix products, update(): jnp.einsum('eva,ael->evl', weights.astype(jnp.bfloat16), value_heads, pre...  22.7 us
    all_to_all x1, starting transfers between devices, per_device(): lax.all_to_all(lax.all_to_all(buckets, 'head', split_axis=1, concat_axis=...  21.1 us
    all_to_all x2, local copies, waits for them, and re-layouts, per_device(): lax.all_to_all(lax.all_to_all(buckets, 'head', split_axis=1, concat_axis=...  18.1 us
    dynamic_slice x8, local copies, waits for them, and re-layouts, key_step(): lax.dynamic_slice_in_dim(piece_values, first_row, KEY_BLOCK, 0)  15.8 us
  transfers between devices with their start and end apart: 4, of which 3 were waited for; matrix products, arithmetic and copies ran while one was open for 26% of the time, Pallas kernels for 0%

profile of v1, /device:TPU:96, one launch (start us, length us, event | category | flops | bytes accessed | tf_op | source)
XLA Modules:
  0.0 539.0 jit_solution(14633590088818679633)
XLA Ops:
  7.2 0.9 reduce-window.4
  8.1 0.7 fusion.29
  8.8 1.5 copy.61
  10.3 0.8 select_reduce_fusion
  11.1 0.5 multiply_cosine_fusion
  11.6 0.3 fusion.21
  12.0 0.6 copy.66
  12.6 1.4 pad_maximum_fusion
  14.0 2.8 copy.67
  16.8 3.5 broadcast_select_fusion
  20.3 5.7 %all-to-all-start.1 = ((bf16[2,4,256,1792]{2,3,0,1:T(8,128)(2,1)}), bf16[2,4,256,1792]{2,3,0,1:T(8,128)(2,1)}, u32[]{:S(2)}, u32[]{:S(2)}) async-start(bf16[2,4,256,1792]{2,3,0,1:T(8,128)(2,1)} %broadcast_select_fusion), calls=%async_computation.1 | async-start | bytes 14680064 | tf_op jit(solution)/shard_map/all_to_all | solution.py:144
  25.9 0.5 copy.63
  26.5 82.9 %all-to-all-done.1 = bf16[2,4,256,1792]{2,3,0,1:T(8,128)(2,1)} async-done(((bf16[2,4,256,1792]{2,3,0,1:T(8,128)(2,1)}), bf16[2,4,256,1792]{2,3,0,1:T(8,128)(2,1)}, u32[]{:S(2)}, u32[]{:S(2)}) %all-to-all-start.1) | async-done | bytes 7340064 | tf_op jit(solution)/shard_map/all_to_all | solution.py:144
  109.4 3.4 stack.6
  112.8 7.8 %all-to-all-start = ((bf16[8,256,1792]{1,2,0:T(8,128)(2,1)}), bf16[8,256,1792]{1,2,0:T(8,128)(2,1)}, u32[]{:S(2)}, u32[]{:S(2)}) async-start(bf16[8,256,1792]{1,2,0:T(8,128)(2,1)} %stack.6), calls=%async_computation | async-start | bytes 14680064 | tf_op jit(solution)/shard_map/all_to_all | solution.py:116
  120.6 0.7 all-gather.2.cloned.1.call-update
  121.4 0.5 copy.62
  121.9 0.6 fusion.27
  122.6 1.3 fusion.28
  125.8 0.3 fusion.24
  126.2 3.6 copy.68
  129.7 47.2 %copy.69 = bf16[2,1,256,7168]{2,0,1,3:T(2,128)(2,1)} copy(bf16[2,1,256,7168]{2,3,0,1:T(8,128)(2,1)S(1)} %bitcast.75) | data formatting | bytes 14680064 | tf_op jit(solution)/shard_map/all_to_all | solution.py:144
  176.9 151.4 %all-to-all-done = bf16[8,256,1792]{1,2,0:T(8,128)(2,1)} async-done(((bf16[8,256,1792]{1,2,0:T(8,128)(2,1)}), bf16[8,256,1792]{1,2,0:T(8,128)(2,1)}, u32[]{:S(2)}, u32[]{:S(2)}) %all-to-all-start) | async-done | bytes 7340064 | tf_op jit(solution)/shard_map/all_to_all | solution.py:116
  328.4 21.1 %all-to-all-start.2 = ((bf16[2,1,256,7168]{2,0,1,3:T(2,128)(2,1)}), bf16[2,1,256,7168]{2,0,1,3:T(2,128)(2,1)}, u32[]{:S(2)}, u32[]{:S(2)}) async-start(bf16[2,1,256,7168]{2,0,1,3:T(2,128)(2,1)} %copy.69), calls=%async_computation.2 | async-start | bytes 14680064 | tf_op jit(solution)/shard_map/all_to_all | solution.py:143
  349.5 10.1 %copy.64 = bf16[8,256,1792]{2,1,0:T(8,128)(2,1)} copy(bf16[8,256,1792]{1,2,0:T(8,128)(2,1)} %all-to-all-done) | data formatting | bytes 14680064 | tf_op jit(solution)/shard_map/all_to_all | solution.py:116
  359.6 72.1 %while.18 = (s32[]{:T(128)}, f32[8,256]{1,0:T(8,128)S(1)}, f32[8,256]{1,0:T(8,128)S(1)}, f32[8,256,224]{1,2,0:T(8,128)}, s32[4]{0:T(128)S(1)}, /*index=5*/s32[25...) while((s32[]{:T(128)}, f32[8,256]{1,0:T(8,128)S(1)}, ...), condition=%wide.region_8.9_spmd.clone, body=%wide.region_4.8_spmd.clone.sunk | while | flops 955204608 | bytes 32524004 | solution.py:133
  359.6 0.1 convert_reduce_fusion.3
  359.7 0.3 and_or_fusion.2
  360.0 1.6 constant_dynamic-slice_fusion.4
  361.6 3.2 fusion.45
  364.8 3.2 fusion.46
  368.0 1.6 constant_dynamic-slice_fusion.5
  369.6 2.3 copy.78
  371.9 5.3 fusion.48
  377.2 0.1 convert_reduce_fusion.3
  377.3 0.3 and_or_fusion.2
  377.6 1.6 constant_dynamic-slice_fusion.4
  379.2 3.2 fusion.45
  382.4 3.2 fusion.46
  385.6 1.6 constant_dynamic-slice_fusion.5
  387.2 2.3 copy.78
  389.6 5.8 %fusion.48 = f32[8,256,224]{1,2,0:T(8,128)} fusion(f32[8,256,224]{1,2,0:T(8,128)} %get-tuple-element.367, bf16[512,8,224]{0,2,1:T(8,128)(2,1)} %bitcast.72, f32[8,512,256]{2,1,0:T(8,128)} %get-tuple-element.347, f32[8,256]{1,0:T(8,128)S(1)} %select_maximum_fusion.2, pred[256,512]{0,1:T(8,128)(4,1)S(1)} %and_or_fusion.2, ...), kind=kOutput, calls=%fused_computation.13.clone.1 | convolution fusion | flops 476381184 | bytes 9846785 | tf_op jit(solution)/shard_map/while/body/eval_jaxpr/eva,ael->evl/dot_general | solution.py:85
  395.4 0.1 convert_reduce_fusion.3
  395.5 0.3 and_or_fusion.2
  395.8 1.6 constant_dynamic-slice_fusion.4
  397.4 3.2 fusion.45
  400.6 3.2 fusion.46
  403.8 1.6 constant_dynamic-slice_fusion.5
  405.4 2.3 copy.78
  407.7 5.8 %fusion.48 = f32[8,256,224]{1,2,0:T(8,128)} fusion(f32[8,256,224]{1,2,0:T(8,128)} %get-tuple-element.367, bf16[512,8,224]{0,2,1:T(8,128)(2,1)} %bitcast.72, f32[8,512,256]{2,1,0:T(8,128)} %get-tuple-element.347, f32[8,256]{1,0:T(8,128)S(1)} %select_maximum_fusion.2, pred[256,512]{0,1:T(8,128)(4,1)S(1)} %and_or_fusion.2, ...), kind=kOutput, calls=%fused_computation.13.clone.1 | convolution fusion | flops 476381184 | bytes 9846785 | tf_op jit(solution)/shard_map/while/body/eval_jaxpr/eva,ael->evl/dot_general | solution.py:85
  413.5 0.1 convert_reduce_fusion.3
  413.6 0.3 and_or_fusion.2
  413.9 1.6 constant_dynamic-slice_fusion.4
  415.5 3.2 fusion.45
  418.7 3.2 fusion.46
  421.9 1.6 constant_dynamic-slice_fusion.5
  423.6 2.3 copy.78
  425.9 5.8 %fusion.48 = f32[8,256,224]{1,2,0:T(8,128)} fusion(f32[8,256,224]{1,2,0:T(8,128)} %get-tuple-element.367, bf16[512,8,224]{0,2,1:T(8,128)(2,1)} %bitcast.72, f32[8,512,256]{2,1,0:T(8,128)} %get-tuple-element.347, f32[8,256]{1,0:T(8,128)S(1)} %select_maximum_fusion.2, pred[256,512]{0,1:T(8,128)(4,1)S(1)} %and_or_fusion.2, ...), kind=kOutput, calls=%fused_computation.13.clone.1 | convolution fusion | flops 476381184 | bytes 9846785 | tf_op jit(solution)/shard_map/while/body/eval_jaxpr/eva,ael->evl/dot_general | solution.py:85
  431.7 1.6 divide_convert_fusion
  433.3 1.4 copy.72
  434.7 73.8 %all-to-all-done.2 = bf16[2,1,256,7168]{2,0,1,3:T(2,128)(2,1)} async-done(((bf16[2,1,256,7168]{2,0,1,3:T(2,128)(2,1)}), bf16[2,1,256,7168]{2,0,1,3:T(2,128)(2,1)}, u32[]{:S(2)}, u32[]{:S(2)}) %all-to-all-start.2) | async-done | bytes 7340064 | tf_op jit(solution)/shard_map/all_to_all | solution.py:143
  508.5 7.0 %copy.70 = bf16[2,1,256,7168]{2,3,0,1:T(8,128)(2,1)} copy(bf16[2,1,256,7168]{2,0,1,3:T(2,128)(2,1)} %all-to-all-done.2) | data formatting | bytes 14680064 | tf_op jit(solution)/shard_map/all_to_all | solution.py:143
  515.5 11.1 %copy.71 = bf16[2,1,8,256,896]{4,3,2,0,1:T(8,128)(2,1)} copy(bf16[2,1,8,256,896]{3,4,2,0,1:T(8,128)(2,1)} %bitcast.76) | data formatting | bytes 14680064 | tf_op jit(solution)/shard_map/all_to_all | solution.py:143
  526.6 5.6 %fusion.19 = (bf16[1,1,1024,896]{3,2,1,0:T(8,128)(2,1)}, bf16[1,1,1024,896]{3,2,1,0:T(8,128)(2,1)}) fusion(s32[]{:T(128)S(6)} %add.111, s32[]{:T(128)S(6)} %select_n.53, bf16[2,1,2048,896]{3,2,0,1:T(8,128)(2,1)} %bitcast.77), kind=kLoop, calls=%fused_computation.32 | loop fusion | bytes 11010056
  (52 shorter events, 0.4 us)
Async XLA Ops:
  7.2 5.4 %copy-start.1 = (bf16[1,256,1792]{2,1,0:T(8,128)(2,1)S(1)}, bf16[1,256,1792]{2,1,0:T(8,128)(2,1)}, u32[]{:S(2)}) copy-start(bf16[1,256,1792]{2,1,0:T(8,128)(2,1)} %param.10) | copy-start | bytes 2752516
  12.0 4.8 copy-start
  20.3 5.7 %copy-start.2 = (bf16[1,256,1792]{2,1,0:T(8,128)(2,1)S(1)}, bf16[1,256,1792]{2,1,0:T(8,128)(2,1)}, u32[]{:S(2)}) copy-start(bf16[1,256,1792]{2,1,0:T(8,128)(2,1)} %param.10) | copy-start | bytes 2752516
  20.3 89.1 %all-to-all-start.1 = ((bf16[2,4,256,1792]{2,3,0,1:T(8,128)(2,1)}), bf16[2,4,256,1792]{2,3,0,1:T(8,128)(2,1)}, u32[]{:S(2)}, u32[]{:S(2)}) async-start(bf16[2,4,256,1792]{2,3,0,1:T(8,128)(2,1)} %broadcast_select_fusion), calls=%async_computation.1 | async-start | bytes 14680064 | tf_op jit(solution)/shard_map/all_to_all | solution.py:144
  112.8 8.6 %copy-start.3 = (bf16[1,256,1792]{2,1,0:T(8,128)(2,1)S(1)}, bf16[1,256,1792]{2,1,0:T(8,128)(2,1)}, u32[]{:S(2)}) copy-start(bf16[1,256,1792]{2,1,0:T(8,128)(2,1)} %param.8) | copy-start | bytes 2752516
  112.8 9.1 %copy-start.5 = (s32[1,4]{1,0:T(1,128)S(1)}, s32[1,4]{1,0:T(1,128)}, u32[]{:S(2)}) copy-start(s32[1,4]{1,0:T(1,128)} %param.13) | copy-start | bytes 52
  112.8 9.7 %copy-start.4 = (s32[1,4]{1,0:T(1,128)S(1)}, s32[1,4]{1,0:T(1,128)}, u32[]{:S(2)}) copy-start(s32[1,4]{1,0:T(1,128)} %param.11) | copy-start | bytes 52
  112.8 215.6 %all-to-all-start = ((bf16[8,256,1792]{1,2,0:T(8,128)(2,1)}), bf16[8,256,1792]{1,2,0:T(8,128)(2,1)}, u32[]{:S(2)}, u32[]{:S(2)}) async-start(bf16[8,256,1792]{1,2,0:T(8,128)(2,1)} %stack.6), calls=%async_computation | async-start | bytes 14680064 | tf_op jit(solution)/shard_map/all_to_all | solution.py:116
  120.6 239.0 %all-gather.2.cloned.1.call-start = ((), (), s32[]{:S(2)}) async-start(), calls=%async_computation.3 | async-start | bytes 8257536 | tf_op jit(solution)/shard_map/all_gather | solution.py:114
  328.4 180.1 %all-to-all-start.2 = ((bf16[2,1,256,7168]{2,0,1,3:T(2,128)(2,1)}), bf16[2,1,256,7168]{2,0,1,3:T(2,128)(2,1)}, u32[]{:S(2)}, u32[]{:S(2)}) async-start(bf16[2,1,256,7168]{2,0,1,3:T(2,128)(2,1)} %copy.69), calls=%async_computation.2 | async-start | bytes 14680064 | tf_op jit(solution)/shard_map/all_to_all | solution.py:143
Sparse Core Ops, SparseCore 0:
  123.7 229.8 all-gather.1
